TPU v7x, 256 devices: a whole 4x4x8 slice. The times are simulated.
256 devices in a mesh: date: 16 (over z, core), tile: 16 (over x, y).
Axes of the slice: x: 4, y: 4, z: 8, core: 2. Of those that a mesh axis runs over, the one named last changes fastest.
Arguments:
- imagery: bfloat16 [10, 64, 65536], P(None, 'date', 'tile'), may hold values from -6 to 6
- owner: int32 [65536, 1], replicated, may hold values from 0 to 15; in each aligned block of 4096 rows (0 to 4095, 4096 to 8191, ...) at most 1024 rows name the same one
- parcel_local: int32 [65536], replicated, may hold values from 0 to 15
- lift_weight: bfloat16 [10, 128], replicated, may hold values from -2 to 2
- depth_weight: float32 [2, 5, 128], replicated, may hold values from -2.5 to 2.5
- point_weight: bfloat16 [2, 128, 128], replicated, may hold values from -0.5 to 0.5
- bn_mean: float32 [2, 128], replicated, may hold values from -0.5 to 0.5
- bn_var: float32 [2, 128], replicated, may hold values from 0.25 to 4
- bn_gain: float32 [2, 128], replicated, may hold values from 0.5 to 2
- bn_shift: float32 [2, 128], replicated, may hold values from -1 to 1
Outputs:
- parcel_means: float32 [16, 256, 128], P('date', 'tile')
Inputs may be any that keep to these rules, and one draw needn't show every extreme that they name: `owner`: in each aligned block of 4096 rows (the pixels of one tile), no tile index appears more than 1024 times, and some index appears exactly 1024 times.
All inputs are finite; a program needn't handle non-finite values.
Results may differ from a plain program's by a relative error of at most 0.0008.
Values may be sent and summed in bfloat16 or wider, within the bound.
No kernel may reach another device: no remote copies, remote signals or barrier semaphores. Data moves between devices by JAX's collectives and lax.ppermute only.
A program may use at most 128 MiB of HBM per device.

v0:
```python
import math
import jax
import jax.numpy as jnp
from jax import lax
from jax.sharding import PartitionSpec as P

PARC_DEV = 16
epsilon = 1e-05


def layer_stack(series, weights):
    lift_weight, depth_weight, point_weight, bn_mean, bn_var, bn_gain, bn_shift = weights
    hidden = jnp.einsum(
        "bts,bc->tsc", series, lift_weight, preferred_element_type=jnp.float32
    ).astype(jnp.bfloat16)
    for layer in range(depth_weight.shape[0]):
        length = hidden.shape[0]
        half = depth_weight.shape[1] // 2
        widened = jnp.pad(hidden, ((half, half), (0, 0), (0, 0)))
        spread = jnp.zeros(hidden.shape, jnp.float32)
        for tap in range(depth_weight.shape[1]):
            spread = spread + depth_weight[layer, tap] * widened[tap : tap + length]
        spread = spread.astype(jnp.bfloat16)
        mixed = jnp.einsum(
            "tsc,cd->tsd", spread, point_weight[layer], preferred_element_type=jnp.float32
        )
        factor = bn_gain[layer] / jnp.sqrt(bn_var[layer] + epsilon)
        normed = jax.nn.relu((mixed - bn_mean[layer]) * factor + bn_shift[layer])
        hidden = (0.5 * (normed[0::2] + normed[1::2])).astype(jnp.bfloat16)
    return hidden


def local(
    imagery,
    owner,
    parcel_local,
    lift_weight,
    depth_weight,
    point_weight,
    bn_mean,
    bn_var,
    bn_gain,
    bn_shift,
):
    weights = (lift_weight, depth_weight, point_weight, bn_mean, bn_var, bn_gain, bn_shift)
    tiles = lax.axis_size("tile")
    dates = lax.axis_size("date")
    tile_index = lax.axis_index("tile")
    date_index = lax.axis_index("date")
    bands, date_dev, pix_dev = imagery.shape
    owners = owner[:, 0]
    mine = owners == tile_index
    catalog = jnp.arange(PARC_DEV, dtype=jnp.int32)
    counts = jnp.sum(
        ((parcel_local[:, None] == catalog[None, :]) & mine[:, None]).astype(jnp.int32), axis=0
    )
    capacity = 4 * pix_dev // max(tiles, 8)
    share = capacity // dates
    owner_ids = jnp.arange(tiles, dtype=jnp.int32)
    positions = jnp.arange(pix_dev, dtype=jnp.int32)
    own_owner = lax.dynamic_slice_in_dim(owners, tile_index * pix_dev, pix_dev, 0)
    onehot = (own_owner[:, None] == owner_ids[None, :]).astype(jnp.int32)
    running = jnp.cumsum(onehot, axis=0)
    own_rank = jnp.sum(running * onehot, axis=1) - 1
    own_count = jnp.sum(onehot, axis=0)
    table = (
        jnp.zeros((tiles * capacity,), jnp.int32).at[own_owner * capacity + own_rank].set(positions)
    )
    table = table.reshape(tiles, share, dates).transpose(2, 0, 1).reshape(-1)
    rank_send = (
        jnp.arange(share, dtype=jnp.int32)[None, None, :] * dates
        + jnp.arange(dates, dtype=jnp.int32)[:, None, None]
    )
    valid_send = (rank_send < own_count[None, :, None]).reshape(-1)
    rows = imagery.reshape(bands * date_dev, pix_dev).T
    picked = jnp.take(rows, table, axis=0)
    picked = jnp.where(valid_send[:, None], picked, jnp.zeros_like(picked))
    outgoing = picked.T.reshape(bands, date_dev, table.shape[0])
    arrived = lax.all_to_all(
        lax.all_to_all(outgoing, "date", split_axis=2, concat_axis=1, tiled=True),
        "tile",
        split_axis=2,
        concat_axis=2,
        tiled=True,
    )
    grid = owners.reshape(tiles, pix_dev)
    mine_grid = (grid == tile_index).astype(jnp.int32)
    recv_rank = jnp.cumsum(mine_grid, axis=1) - 1
    target = jnp.where(mine_grid == 1, owner_ids[:, None] * capacity + recv_rank, tiles * capacity)
    recv_table = (
        jnp.full((tiles * capacity + 1,), -1, jnp.int32).at[target.reshape(-1)].set(parcel_local)
    )
    slot_ranks = jnp.arange(share, dtype=jnp.int32) * dates + date_index
    slot_parcel = jnp.take(recv_table[:-1].reshape(tiles, capacity), slot_ranks, axis=1).reshape(-1)
    slots = arrived.shape[2]
    block = math.gcd(slots, 512)
    nblocks = slots // block
    pieces = arrived.reshape(bands, arrived.shape[1], nblocks, block).transpose(2, 0, 1, 3)
    labels = slot_parcel.reshape(nblocks, block)

    def run_block(item):
        piece, label = item
        features = layer_stack(piece, weights)
        member = (label[None, :] == catalog[:, None]).astype(jnp.bfloat16)
        return jnp.einsum("qs,jsc->jqc", member, features, preferred_element_type=jnp.float32)

    partial_value = jnp.sum(lax.map(run_block, (pieces, labels)), axis=0)
    sums = lax.psum_scatter(partial_value, "date", scatter_dimension=0, tiled=True)
    return sums / jnp.maximum(counts, 1).astype(jnp.float32)[None, :, None]


def solution(mesh):
    placed = (P(None, "date", "tile"), P(), P(), P(), P(), P(), P(), P(), P(), P())
    return jax.shard_map(
        local, mesh=mesh, in_specs=placed, out_specs=P("date", "tile", None), check_vma=False
    )
```

profile of v0, /device:TPU:4, one launch (start us, length us, event | category | flops | bytes accessed | tf_op | source)
XLA Modules:
  0.0 670.8 jit_solution(5873517295143704459)
XLA Ops:
  6.5 0.7 constant_dynamic-slice_fusion.1
  7.3 4.6 reduce-window.14
  11.9 0.5 slice_reduce_fusion.1
  13.0 0.8 compare_select_fusion.4
  13.7 15.6 %scatter_custom_fusion = s32[16384]{0:T(1024)S(1)} fusion(s32[4096]{0:T(1024)S(1)} %bitcast.142, s32[4096]{0:T(1024)S(1)} %iota.39, s32[]{:T(128)} %copy.70), kind=kCustom, calls=%fused_computation.86 | custom fusion | bytes 65540 | tf_op jit(solution)/shard_map/scatter | solution.py:67
  30.1 1.1 reshape.262
  31.3 0.5 copy.47
  31.8 57.4 %gather_fusion = bf16[16384,40]{1,0:T(8,128)(2,1)} fusion(bf16[4096,40]{1,0:T(8,128)(2,1)S(1)} %bitcast.121, s32[16384]{0:T(1024)S(1)} %broadcast_clamp_fusion), kind=kCustom, calls=%fused_computation | custom fusion | bytes 2686976 | tf_op jit(solution)/shard_map/jit(_take)/gather | solution.py:76
  89.2 13.9 %select_bitcast_fusion = bf16[40,16384]{0,1:T(8,128)(2,1)} fusion(bf16[16384,40]{1,0:T(8,128)(2,1)} %gather_fusion, pred[16384]{0:T(1024)(128)(4,1)S(1)} %compare_and_fusion, pred[16384]{0:T(1024)(128)(4,1)S(1)} %lt.84), kind=kLoop, calls=%fused_computation.60 | loop fusion | flops 1310720 | bytes 2654208 | tf_op jit(solution)/shard_map/jit(_where)/select_n | solution.py:77
  103.1 3.5 copy.49
  106.6 0.5 reshape.264
  107.1 16.3 %copy.50 = bf16[10,4,16384]{0,1,2:T(4,128)(2,1)} copy(bf16[10,4,16384]{2,1,0:T(4,128)(2,1)S(1)} %reshape.264) | data formatting | bytes 2621440 | tf_op jit(solution)/shard_map/reshape | solution.py:78
  123.4 27.2 %reshape.312 = bf16[16,2,20480]{2,1,0:T(2,128)(2,1)} reshape(bf16[16384,4,10]{2,1,0:T(4,128)(2,1)} %bitcast.122) | data formatting | bytes 2621440
  150.6 8.6 %all-to-all-start = ((bf16[16,2,20480]{2,1,0:T(2,128)(2,1)}), bf16[16,2,20480]{2,1,0:T(2,128)(2,1)S(1)}, u32[]{:S(2)}, u32[]{:S(2)}) async-start(bf16[16,2,20480]{2,1,0:T(2,128)(2,1)} %reshape.312), calls=%async_computation | async-start | bytes 2621440 | tf_op jit(solution)/shard_map/all_to_all | solution.py:80
  159.3 0.3 copy.60
  159.6 1.4 compare_reduce_fusion
  161.0 4.6 reduce-window.16
  165.6 0.5 slice_reduce_fusion
  166.4 24.9 %all-to-all-done = bf16[16,2,20480]{2,1,0:T(2,128)(2,1)S(1)} async-done(((bf16[16,2,20480]{2,1,0:T(2,128)(2,1)}), bf16[16,2,20480]{2,1,0:T(2,128)(2,1)S(1)}, u32[]{:S(2)}, u32[]{:S(2)}) %all-to-all-start) | async-done | bytes 1310752 | tf_op jit(solution)/shard_map/all_to_all | solution.py:80
  191.4 40.8 %reshape.313 = bf16[16384,4,10]{2,1,0:T(4,128)(2,1)} reshape(bf16[16,2,20480]{2,1,0:T(2,128)(2,1)S(1)} %all-to-all-done) | data formatting | bytes 2621440
  232.2 23.6 %copy.51 = bf16[10,4,16,1024]{3,1,2,0:T(4,128)(2,1)S(1)} copy(bf16[10,4,16,1024]{0,1,3,2:T(4,128)(2,1)} %bitcast.123) | data formatting | bytes 2621440 | tf_op jit(solution)/shard_map/all_to_all | solution.py:80
  255.8 0.3 all_to_all.19
  256.1 4.8 copy.52
  260.9 6.5 reshape.314
  267.5 7.5 %all-to-all-start.1 = ((bf16[16,2,20480]{2,1,0:T(2,128)(2,1)}), bf16[16,2,20480]{2,1,0:T(2,128)(2,1)S(1)}, u32[]{:S(2)}, u32[]{:S(2)}) async-start(bf16[16,2,20480]{2,1,0:T(2,128)(2,1)} %reshape.314), calls=%async_computation.1 | async-start | bytes 2621440 | tf_op jit(solution)/shard_map/all_to_all | solution.py:79
  275.0 0.6 compare_select_fusion
  275.7 240.0 %scatter_custom_fusion.1 = s32[16385]{0:T(1024)S(1)} fusion(s32[65536]{0:T(1024)S(1)} %bitcast.134, s32[65536]{0:T(1024)} %param.14, s32[]{:T(128)} %constant.109.clone.1), kind=kCustom, calls=%fused_computation.83 | custom fusion | bytes 66052 | tf_op jit(solution)/shard_map/scatter | solution.py:91
  516.1 0.6 gather_fusion.1
  516.8 3.6 reshape.315
  520.5 7.4 %copy.58 = bf16[10,64,2,512]{3,2,1,0:T(2,128)(2,1)S(1)} copy(bf16[10,64,2,512]{1,0,3,2:T(8,128)(2,1)} %bitcast.125) | data formatting | bytes 2621440 | tf_op jit(solution)/shard_map/reshape | solution.py:98
  527.8 0.8 copy.57
  528.7 77.0 %while.13 = (s32[]{:T(128)}, f32[2,16,16,128]{3,2,1,0:T(8,128)}, f32[2,5,128]{2,1,0:T(8,128)S(1)}, bf16[2,10,64,512]{3,1,2,0:T(8,128)(2,1)S(1)}, bf16[10,128]{1,...) while((s32[]{:T(128)}, f32[2,16,16,128]{3,2,1,0:T(8,128)}, ...), condition=%wide.region_9.10_spmd.clone, body=%wide.region_8.9_spmd.clone.sunk | while | flops 1861231104 | bytes 78875824 | solution.py:107
  529.0 4.7 convolution_convert_fusion.2
  533.7 21.0 %add_maximum_fusion.4 = f32[64,512,128]{2,1,0:T(8,128)} fusion(f32[128]{0:T(128)S(1)} %get-tuple-element.364, f32[128]{0:T(128)S(1)} %get-tuple-element.365, f32[128]{0:T(128)S(1)} %get-tuple-element.366, bf16[64,512,128]{2,1,0:T(8,128)(2,1)} %convolution_convert_fusion.2, f32[128]{0:T(128)S(1)} %get-tuple-element.367, ...), kind=kOutput, calls=%fused_computation.5.clone.1 | convolution fusion | flops 1153433600 | bytes 25202688 | tf_op jit(solution)/shard_map/while/body/eval_jaxpr/tsc,cd->tsd/dot_general | solution.py:24
  554.8 6.4 multiply_convert_fusion.10
  561.2 4.9 add_maximum_fusion.5
  566.2 0.5 fusion.47
  566.6 0.7 copy-done.3
  567.4 4.7 convolution_convert_fusion.2
  572.1 21.0 %add_maximum_fusion.4 = f32[64,512,128]{2,1,0:T(8,128)} fusion(f32[128]{0:T(128)S(1)} %get-tuple-element.364, f32[128]{0:T(128)S(1)} %get-tuple-element.365, f32[128]{0:T(128)S(1)} %get-tuple-element.366, bf16[64,512,128]{2,1,0:T(8,128)(2,1)} %convolution_convert_fusion.2, f32[128]{0:T(128)S(1)} %get-tuple-element.367, ...), kind=kOutput, calls=%fused_computation.5.clone.1 | convolution fusion | flops 1153433600 | bytes 25202688 | tf_op jit(solution)/shard_map/while/body/eval_jaxpr/tsc,cd->tsd/dot_general | solution.py:24
  593.1 6.4 multiply_convert_fusion.10
  599.6 4.9 add_maximum_fusion.5
  604.5 0.5 fusion.47
  605.0 0.7 copy-done.3
  605.7 1.6 reduce_sum.38
  607.4 0.8 convert_reduce_fusion
  608.1 54.4 %reduce-scatter.2.cloned.1.call-done = f32[1,16,128]{2,1,0:T(8,128)} async-done(((f32[16,16,128]{2,1,0:T(8,128)}), f32[1,16,128]{2,1,0:T(8,128)}) %reduce-scatter.2.cloned.1.call-update) | async-done | bytes 8208 | tf_op jit(solution)/shard_map/reduce_scatter | solution.py:108
  662.6 1.4 broadcast_divide_fusion
  (72 shorter events, 2.6 us)
Async XLA Ops:
  123.4 36.2 %copy-start = (s32[65536,1]{0,1:T(1,128)S(1)}, s32[65536,1]{0,1:T(1,128)}, u32[]{:S(2)}) copy-start(s32[65536,1]{0,1:T(1,128)} %param.13) | copy-start | bytes 786436
  150.6 40.8 %all-to-all-start = ((bf16[16,2,20480]{2,1,0:T(2,128)(2,1)}), bf16[16,2,20480]{2,1,0:T(2,128)(2,1)S(1)}, u32[]{:S(2)}, u32[]{:S(2)}) async-start(bf16[16,2,20480]{2,1,0:T(2,128)(2,1)} %reshape.312), calls=%async_computation | async-start | bytes 2621440 | tf_op jit(solution)/shard_map/all_to_all | solution.py:80
  255.8 20.0 %copy-start.10 = (f32[2,5,128]{2,0,1:T(2,128)S(1)}, f32[2,5,128]{2,0,1:T(2,128)}, u32[]{:S(2)}) copy-start(f32[2,5,128]{2,0,1:T(2,128)} %param.16) | copy-start | bytes 15364
  267.5 249.3 %all-to-all-start.1 = ((bf16[16,2,20480]{2,1,0:T(2,128)(2,1)}), bf16[16,2,20480]{2,1,0:T(2,128)(2,1)S(1)}, u32[]{:S(2)}, u32[]{:S(2)}) async-start(bf16[16,2,20480]{2,1,0:T(2,128)(2,1)} %reshape.314), calls=%async_computation.1 | async-start | bytes 2621440 | tf_op jit(solution)/shard_map/all_to_all | solution.py:79
  274.9 253.7 %copy-start.5 = (bf16[10,128]{1,0:T(8,128)(2,1)S(1)}, bf16[10,128]{1,0:T(8,128)(2,1)}, u32[]{:S(2)}) copy-start(bf16[10,128]{1,0:T(8,128)(2,1)} %param.15) | copy-start | bytes 7684
  274.9 253.7 %copy-start.6 = (f32[2,128]{1,0:T(2,128)S(1)}, f32[2,128]{1,0:T(2,128)}, u32[]{:S(2)}) copy-start(f32[2,128]{1,0:T(2,128)} %param.20) | copy-start | bytes 3076
  274.9 253.7 %copy-start.7 = (f32[2,128]{1,0:T(2,128)S(1)}, f32[2,128]{1,0:T(2,128)}, u32[]{:S(2)}) copy-start(f32[2,128]{1,0:T(2,128)} %param.19) | copy-start | bytes 3076
  275.0 253.7 %copy-start.8 = (f32[2,128]{1,0:T(2,128)S(1)}, f32[2,128]{1,0:T(2,128)}, u32[]{:S(2)}) copy-start(f32[2,128]{1,0:T(2,128)} %param.21) | copy-start | bytes 3076
  275.0 253.7 %copy-start.9 = (f32[2,128]{1,0:T(2,128)S(1)}, f32[2,128]{1,0:T(2,128)}, u32[]{:S(2)}) copy-start(f32[2,128]{1,0:T(2,128)} %param.18) | copy-start | bytes 3076
  275.0 253.7 %copy-start.11 = (bf16[2,128,128]{2,1,0:T(8,128)(2,1)S(1)}, bf16[2,128,128]{2,1,0:T(8,128)(2,1)}, u32[]{:S(2)}) copy-start(bf16[2,128,128]{2,1,0:T(8,128)(2,1)} %param.17) | copy-start | bytes 196612
  275.0 387.6 %reduce-scatter.2.cloned.1.call-start = ((), (), s32[]{:S(2)}) async-start(), calls=%async_computation.3 | async-start | bytes 139264 | tf_op jit(solution)/shard_map/reduce_scatter | solution.py:108
  528.7 78.7 %copy-start.1 = (s32[65536]{0:T(1024)S(1)}, s32[65536]{0:T(1024)}, u32[]{:S(2)}) copy-start(s32[65536]{0:T(1024)} %param.14) | copy-start | bytes 786436
  528.7 78.6 %copy-start.4 = (pred[65536]{0:T(1024)(128)(4,1)S(1)}, pred[65536]{0:T(1024)(128)(4,1)}, u32[]{:S(2)}) copy-start(pred[65536]{0:T(1024)(128)(4,1)} %get-tuple-element.276) | copy-start | bytes 196612
  561.2 5.0 copy-start.2
  566.6 0.7 copy-start.3
  599.6 5.0 copy-start.2
  605.0 0.7 copy-start.3
Sparse Core Ops, SparseCore 0:
  607.5 55.0 reduce-scatter.1
where the time goes:
time: 672 us; the launch traced here: 671 us
  local copies, waits for them, and re-layouts  455 us (68%)
  waiting for transfers between devices  79.4 us (12%)
  matrix products  62.3 us (9%)
  other arithmetic  43.7 us (7%)
  starting transfers between devices  16.1 us (2%)
  between operations  13.8 us (2%)
    scatter x1, local copies, waits for them, and re-layouts, local(): jnp.full((tiles * capacity + 1,), -1, jnp.int32).at[target.reshape(-1)]  240 us
    unnamed x28, local copies, waits for them, and re-layouts  79.4 us
    gather x1, local copies, waits for them, and re-layouts, local(): picked = jnp.take(rows, table, axis=0)  57.4 us
    reduce_scatter x1, waiting for transfers between devices, local(): lax.psum_scatter(partial_value, 'date', scatter_dimension=0, tiled=True)  54.4 us
    dot_general x4, matrix products, layer_stack(): jnp.einsum('tsc,cd->tsd', spread, point_weight[layer], preferred_element_...  52 us
    all_to_all x3, local copies, waits for them, and re-layouts, local(): lax.all_to_all(outgoing, 'date', split_axis=2, concat_axis=1, tiled=True)  28.7 us
    all_to_all x1, waiting for transfers between devices, local(): lax.all_to_all(outgoing, 'date', split_axis=2, concat_axis=1, tiled=True)  24.9 us
    reshape x2, local copies, waits for them, and re-layouts, local(): outgoing = picked.T.reshape(bands, date_dev, table.shape[0])  16.8 us
  transfers between devices with their start and end apart: 3, of which 2 were waited for; matrix products, arithmetic and copies ran while one was open for 37% of the time, Pallas kernels for 0%

commit v1 on v0

--- a/solution.py
+++ b/solution.py
@@ -76,13 +76,10 @@
     picked = jnp.take(rows, table, axis=0)
     picked = jnp.where(valid_send[:, None], picked, jnp.zeros_like(picked))
     outgoing = picked.T.reshape(bands, date_dev, table.shape[0])
-    arrived = lax.all_to_all(
-        lax.all_to_all(outgoing, "date", split_axis=2, concat_axis=1, tiled=True),
-        "tile",
-        split_axis=2,
-        concat_axis=2,
-        tiled=True,
-    )
+    block_2 = lax.all_to_all(outgoing, "date", split_axis=2, concat_axis=1, tiled=True)
+    parts = jnp.split(block_2, lax.axis_size("tile"), axis=2)
+    arrived_2 = lax.all_to_all(jnp.stack(parts), "tile", 0, 0)
+    arrived = jnp.concatenate(arrived_2, axis=2)
     grid = owners.reshape(tiles, pix_dev)
     mine_grid = (grid == tile_index).astype(jnp.int32)
     recv_rank = jnp.cumsum(mine_grid, axis=1) - 1

time: 672 us -> 679 us (1.010)
  local copies, waits for them, and re-layouts: 455 us -> 462 us
    unnamed x28 -> x43, local copies, waits for them, and re-layouts: 79.4 us -> 89.7 us
    all_to_all x3 -> x2, local copies, waits for them, and re-layouts: 28.7 us -> 23.9 us  [local(): lax.all_to_all(outgoing, 'date', split_axis=2, concat_axis=1, tiled=True)]
where the time goes in v1:
time: 679 us; the launch traced here: 678 us
  local copies, waits for them, and re-layouts  462 us (68%)
  waiting for transfers between devices  79.4 us (12%)
  matrix products  62.3 us (9%)
  other arithmetic  43.7 us (6%)
  starting transfers between devices  16.1 us (2%)
  between operations  13.8 us (2%)
    scatter x1, local copies, waits for them, and re-layouts, local(): jnp.full((tiles * capacity + 1,), -1, jnp.int32).at[target.reshape(-1)]  240 us
    unnamed x43, local copies, waits for them, and re-layouts  89.7 us
    gather x1, local copies, waits for them, and re-layouts, local(): picked = jnp.take(rows, table, axis=0)  57.4 us
    reduce_scatter x1, waiting for transfers between devices, local(): lax.psum_scatter(partial_value, 'date', scatter_dimension=0, tiled=True)  54.4 us
    dot_general x4, matrix products, layer_stack(): jnp.einsum('tsc,cd->tsd', spread, point_weight[layer], preferred_element_...  52 us
    all_to_all x1, waiting for transfers between devices, local(): lax.all_to_all(outgoing, 'date', split_axis=2, concat_axis=1, tiled=True)  24.9 us
    all_to_all x2, local copies, waits for them, and re-layouts, local(): lax.all_to_all(outgoing, 'date', split_axis=2, concat_axis=1, tiled=True)  23.9 us
    reshape x2, local copies, waits for them, and re-layouts, local(): outgoing = picked.T.reshape(bands, date_dev, table.shape[0])  16.8 us
  transfers between devices with their start and end apart: 3, of which 2 were waited for; matrix products, arithmetic and copies ran while one was open for 37% of the time, Pallas kernels for 0%

profile of v1, /device:TPU:4, one launch (start us, length us, event | category | flops | bytes accessed | tf_op | source)
XLA Modules:
  0.0 677.6 jit_solution(17209050162481803014)
XLA Ops:
  6.5 0.7 constant_dynamic-slice_fusion.1
  7.3 4.6 reduce-window.14
  13.0 0.8 compare_select_fusion.4
  13.7 15.6 %scatter_custom_fusion = s32[16384]{0:T(1024)S(1)} fusion(s32[4096]{0:T(1024)S(1)} %bitcast.205, s32[4096]{0:T(1024)S(1)} %iota.39, s32[]{:T(128)} %copy.82), kind=kCustom, calls=%fused_computation.118 | custom fusion | bytes 65540 | tf_op jit(solution)/shard_map/scatter | solution.py:67
  30.1 1.1 reshape.262
  31.8 57.4 %gather_fusion = bf16[16384,40]{1,0:T(8,128)(2,1)} fusion(bf16[4096,40]{1,0:T(8,128)(2,1)S(1)} %bitcast.185, s32[16384]{0:T(1024)S(1)} %broadcast_clamp_fusion), kind=kCustom, calls=%fused_computation | custom fusion | bytes 2686976 | tf_op jit(solution)/shard_map/jit(_take)/gather | solution.py:76
  89.2 13.9 %select_bitcast_fusion = bf16[40,16384]{0,1:T(8,128)(2,1)} fusion(bf16[16384,40]{1,0:T(8,128)(2,1)} %gather_fusion, pred[16384]{0:T(1024)(128)(4,1)S(1)} %compare_and_fusion, pred[16384]{0:T(1024)(128)(4,1)S(1)} %lt.84), kind=kLoop, calls=%fused_computation.60 | loop fusion | flops 1310720 | bytes 2654208 | tf_op jit(solution)/shard_map/jit(_where)/select_n | solution.py:77
  103.1 3.5 copy.48
  107.1 16.3 %copy.49 = bf16[10,4,16384]{0,1,2:T(4,128)(2,1)} copy(bf16[10,4,16384]{2,1,0:T(4,128)(2,1)S(1)} %reshape.264) | data formatting | bytes 2621440 | tf_op jit(solution)/shard_map/reshape | solution.py:78
  123.4 27.2 %reshape.312 = bf16[16,2,20480]{2,1,0:T(2,128)(2,1)} reshape(bf16[16384,4,10]{2,1,0:T(4,128)(2,1)} %bitcast.186) | data formatting | bytes 2621440
  150.6 8.6 %all-to-all-start = ((bf16[16,2,20480]{2,1,0:T(2,128)(2,1)}), bf16[16,2,20480]{2,1,0:T(2,128)(2,1)S(1)}, u32[]{:S(2)}, u32[]{:S(2)}) async-start(bf16[16,2,20480]{2,1,0:T(2,128)(2,1)} %reshape.312), calls=%async_computation | async-start | bytes 2621440 | tf_op jit(solution)/shard_map/all_to_all | solution.py:79
  159.6 1.4 compare_reduce_fusion
  161.0 4.6 reduce-window.16
  166.4 24.9 %all-to-all-done = bf16[16,2,20480]{2,1,0:T(2,128)(2,1)S(1)} async-done(((bf16[16,2,20480]{2,1,0:T(2,128)(2,1)}), bf16[16,2,20480]{2,1,0:T(2,128)(2,1)S(1)}, u32[]{:S(2)}, u32[]{:S(2)}) %all-to-all-start) | async-done | bytes 1310752 | tf_op jit(solution)/shard_map/all_to_all | solution.py:79
  191.4 40.8 %reshape.313 = bf16[16384,4,10]{2,1,0:T(4,128)(2,1)} reshape(bf16[16,2,20480]{2,1,0:T(2,128)(2,1)S(1)} %all-to-all-done) | data formatting | bytes 2621440
  232.2 23.6 %copy.50 = bf16[10,4,16,1024]{3,1,2,0:T(4,128)(2,1)S(1)} copy(bf16[10,4,16,1024]{0,1,3,2:T(4,128)(2,1)} %bitcast.187) | data formatting | bytes 2621440 | tf_op jit(solution)/shard_map/all_to_all | solution.py:79
  256.8 0.8 fusion.45
  258.3 0.8 fusion.43
  259.7 0.8 fusion.41
  260.5 0.7 fusion.40
  261.2 0.8 fusion.39
  262.0 0.7 fusion.38
  262.7 0.8 fusion.37
  263.5 0.7 fusion.36
  264.2 0.8 fusion.35
  265.7 0.8 fusion.33
  267.2 0.8 fusion.31
  268.0 5.2 reshape.314
  273.2 7.5 %all-to-all-start.1 = ((bf16[16,2,20480]{2,1,0:T(2,128)(2,1)}), bf16[16,2,20480]{2,1,0:T(2,128)(2,1)}, u32[]{:S(2)}, u32[]{:S(2)}) async-start(bf16[16,2,20480]{2,1,0:T(2,128)(2,1)} %reshape.314), calls=%async_computation.1 | async-start | bytes 2621440 | tf_op jit(solution)/shard_map/all_to_all | solution.py:81
  281.4 240.3 %scatter_custom_fusion.1 = s32[16385]{0:T(1024)S(1)} fusion(s32[65536]{0:T(1024)S(1)} %bitcast.197, s32[65536]{0:T(1024)} %param.14, s32[]{:T(128)} %constant.109.clone.1), kind=kCustom, calls=%fused_computation.115 | custom fusion | bytes 66052 | tf_op jit(solution)/shard_map/scatter | solution.py:88
  522.7 4.3 reshape.315
  526.9 3.5 copy.51
  530.5 4.2 reshape_reshape.4
  534.6 0.8 copy.55
  535.5 77.0 %while.13 = (s32[]{:T(128)}, f32[2,16,16,128]{3,2,1,0:T(8,128)}, f32[2,5,128]{2,1,0:T(8,128)S(1)}, bf16[2,10,64,512]{3,1,2,0:T(8,128)(2,1)S(1)}, bf16[10,128]{1,...) while((s32[]{:T(128)}, f32[2,16,16,128]{3,2,1,0:T(8,128)}, ...), condition=%wide.region_9.10_spmd.clone, body=%wide.region_8.9_spmd.clone.sunk | while | flops 1861231104 | bytes 78875824 | solution.py:104
  535.9 4.7 convolution_convert_fusion.2
  540.6 21.0 %add_maximum_fusion.4 = f32[64,512,128]{2,1,0:T(8,128)} fusion(f32[128]{0:T(128)S(1)} %get-tuple-element.364, f32[128]{0:T(128)S(1)} %get-tuple-element.365, f32[128]{0:T(128)S(1)} %get-tuple-element.366, bf16[64,512,128]{2,1,0:T(8,128)(2,1)} %convolution_convert_fusion.2, f32[128]{0:T(128)S(1)} %get-tuple-element.367, ...), kind=kOutput, calls=%fused_computation.5.clone.1 | convolution fusion | flops 1153433600 | bytes 25202688 | tf_op jit(solution)/shard_map/while/body/eval_jaxpr/tsc,cd->tsd/dot_general | solution.py:24
  561.6 6.4 multiply_convert_fusion.10
  568.0 4.9 add_maximum_fusion.5
  573.5 0.7 copy-done.3
  574.2 4.7 convolution_convert_fusion.2
  578.9 21.0 %add_maximum_fusion.4 = f32[64,512,128]{2,1,0:T(8,128)} fusion(f32[128]{0:T(128)S(1)} %get-tuple-element.364, f32[128]{0:T(128)S(1)} %get-tuple-element.365, f32[128]{0:T(128)S(1)} %get-tuple-element.366, bf16[64,512,128]{2,1,0:T(8,128)(2,1)} %convolution_convert_fusion.2, f32[128]{0:T(128)S(1)} %get-tuple-element.367, ...), kind=kOutput, calls=%fused_computation.5.clone.1 | convolution fusion | flops 1153433600 | bytes 25202688 | tf_op jit(solution)/shard_map/while/body/eval_jaxpr/tsc,cd->tsd/dot_general | solution.py:24
  600.0 6.4 multiply_convert_fusion.10
  606.4 4.9 add_maximum_fusion.5
  612.6 1.6 reduce_sum.38
  614.2 0.8 convert_reduce_fusion
  615.0 54.4 %reduce-scatter.2.cloned.1.call-done = f32[1,16,128]{2,1,0:T(8,128)} async-done(((f32[16,16,128]{2,1,0:T(8,128)}), f32[1,16,128]{2,1,0:T(8,128)}) %reduce-scatter.2.cloned.1.call-update) | async-done | bytes 8208 | tf_op jit(solution)/shard_map/reduce_scatter | solution.py:105
  669.4 1.4 broadcast_divide_fusion
  (88 shorter events, 11.4 us)
Async XLA Ops:
  123.4 36.2 %copy-start = (s32[65536,1]{0,1:T(1,128)S(1)}, s32[65536,1]{0,1:T(1,128)}, u32[]{:S(2)}) copy-start(s32[65536,1]{0,1:T(1,128)} %param.13) | copy-start | bytes 786436
  150.6 40.8 %all-to-all-start = ((bf16[16,2,20480]{2,1,0:T(2,128)(2,1)}), bf16[16,2,20480]{2,1,0:T(2,128)(2,1)S(1)}, u32[]{:S(2)}, u32[]{:S(2)}) async-start(bf16[16,2,20480]{2,1,0:T(2,128)(2,1)} %reshape.312), calls=%async_computation | async-start | bytes 2621440 | tf_op jit(solution)/shard_map/all_to_all | solution.py:79
  266.5 14.9 %copy-start.10 = (f32[2,5,128]{2,0,1:T(2,128)S(1)}, f32[2,5,128]{2,0,1:T(2,128)}, u32[]{:S(2)}) copy-start(f32[2,5,128]{2,0,1:T(2,128)} %param.16) | copy-start | bytes 15364
  273.2 249.5 %all-to-all-start.1 = ((bf16[16,2,20480]{2,1,0:T(2,128)(2,1)}), bf16[16,2,20480]{2,1,0:T(2,128)(2,1)}, u32[]{:S(2)}, u32[]{:S(2)}) async-start(bf16[16,2,20480]{2,1,0:T(2,128)(2,1)} %reshape.314), calls=%async_computation.1 | async-start | bytes 2621440 | tf_op jit(solution)/shard_map/all_to_all | solution.py:81
  280.6 388.8 %reduce-scatter.2.cloned.1.call-start = ((), (), s32[]{:S(2)}) async-start(), calls=%async_computation.3 | async-start | bytes 139264 | tf_op jit(solution)/shard_map/reduce_scatter | solution.py:105
  530.4 5.0 copy-start.5
  530.4 5.1 copy-start.6
  530.4 5.1 copy-start.7
  530.4 5.1 copy-start.8
  530.4 5.1 copy-start.9
  530.4 5.1 copy-start.11
  535.5 78.7 %copy-start.1 = (s32[65536]{0:T(1024)S(1)}, s32[65536]{0:T(1024)}, u32[]{:S(2)}) copy-start(s32[65536]{0:T(1024)} %param.14) | copy-start | bytes 786436
  535.5 78.7 %copy-start.4 = (pred[65536]{0:T(1024)(128)(4,1)S(1)}, pred[65536]{0:T(1024)(128)(4,1)}, u32[]{:S(2)}) copy-start(pred[65536]{0:T(1024)(128)(4,1)} %get-tuple-element.276) | copy-start | bytes 196612
  568.0 5.0 copy-start.2
  573.5 0.7 copy-start.3
  606.4 5.0 copy-start.2
  611.9 0.7 copy-start.3
Sparse Core Ops, SparseCore 0:
  614.3 55.0 reduce-scatter.1
